TPU v7x, 128 devices: a whole 4x4x4 slice. The times are simulated.
128 devices in a mesh: seq: 16 (over y_lo, z, core), tensor: 8 (over x, y_hi).
Axes of the slice: x: 4, y: 4 (y_hi: 2, y_lo: 2; y = y_hi * 2 + y_lo), z: 4, core: 2. Of those that a mesh axis runs over, the one named last changes fastest.
Arguments:
- activations: bfloat16 [1024, 131072], P('tensor', 'seq'), may hold values from -24 to 24
- first_factor: bfloat16 [512, 512], replicated, may hold values from -0.25 to 0.25
- spectral: float32 [1024, 131072], P('tensor', 'seq'), may hold values from -4 to 4
- second_factor: float32 [256, 256], replicated, may hold values from -0.375 to 0.375
- gate_scale: float32 [1024], replicated, may hold values from -4 to 4
- gate_shift: float32 [1024], replicated, may hold values from -4 to 4
- expand_weight: bfloat16 [1024, 6144], P(None, ('seq', 'tensor')), may hold values from -0.1875 to 0.1875
- reduce_weight: bfloat16 [6144, 1024], P(('seq', 'tensor')), may hold values from -0.3125 to 0.3125
Outputs:
- layer_out: bfloat16 [1024, 131072], P('tensor', 'seq')
All inputs are finite; a program needn't handle non-finite values.
Results may differ from a plain program's by a relative error of at most 0.0052.
Values may be sent and summed in bfloat16 or wider, within the bound.
A program may use at most 128 MiB of HBM per device.

v0:
```python
import jax
import jax.numpy as jnp
from jax import lax
from jax.sharding import PartitionSpec as P

B = 512


epsilon = 1e-06


def normalize(block):
    values = block.astype(jnp.float32)
    scale = lax.rsqrt(jnp.mean(values * values, axis=0, keepdims=True) + epsilon)
    return (values * scale).astype(jnp.bfloat16)


def expand(normed, shard_rows):
    product = jnp.einsum("ch,cl->hl", shard_rows, normed, preferred_element_type=jnp.float32)
    return jax.nn.gelu(product).astype(jnp.bfloat16)


def on_device(
    activations,
    first_factor,
    spectral,
    second_factor,
    gate_scale,
    gate_shift,
    expand_weight,
    reduce_weight,
):
    channels = activations.shape[0]
    blocks = activations.shape[1] // B
    first_pass = jnp.einsum(
        "cai,ij->caj",
        activations.reshape(channels, blocks, B),
        first_factor,
        preferred_element_type=jnp.float32,
    )
    spectrum = first_pass * spectral.reshape(channels, blocks, B)
    mixed_part = jnp.einsum(
        "pa,caj->cpj",
        second_factor,
        lax.all_to_all(spectrum, "seq", split_axis=2, concat_axis=1, tiled=True),
        precision=lax.Precision.HIGHEST,
    )
    returned = lax.all_to_all(mixed_part, "seq", split_axis=1, concat_axis=2, tiled=True)
    offset = lax.axis_index("tensor") * channels
    scale_here = lax.dynamic_slice_in_dim(gate_scale, offset, channels)[:, None]
    shift_here = lax.dynamic_slice_in_dim(gate_shift, offset, channels)[:, None]
    inputs = activations.astype(jnp.float32)
    gating = jax.nn.sigmoid(inputs * scale_here + shift_here)
    residual_in = (inputs + gating * returned.reshape(channels, -1)).astype(jnp.bfloat16)
    token_block = lax.all_to_all(residual_in, "tensor", split_axis=1, concat_axis=0, tiled=True)
    normed = normalize(token_block)
    hidden = expand(normed, lax.all_gather(expand_weight, ("seq", "tensor"), axis=1, tiled=True))
    weight_full = lax.all_gather(reduce_weight, ("seq", "tensor"), axis=0, tiled=True)
    summed = jnp.einsum("hc,hl->cl", weight_full, hidden, preferred_element_type=jnp.float32)
    combined = (token_block.astype(jnp.float32) + summed).astype(jnp.bfloat16)
    return lax.all_to_all(combined, "tensor", split_axis=0, concat_axis=1, tiled=True)


def solution(mesh):
    return jax.shard_map(
        on_device,
        mesh=mesh,
        in_specs=(
            P("tensor", "seq"),
            P(),
            P("tensor", "seq"),
            P(),
            P(),
            P(),
            P(None, ("seq", "tensor")),
            P(("seq", "tensor"), None),
        ),
        out_specs=P("tensor", "seq"),
        check_vma=False,
    )
```

profile of v0, /device:TPU:108, one launch (start us, length us, event | category | flops | bytes accessed | tf_op | source)
XLA Modules:
  0.0 783.2 jit_solution(14307314590979171262)
XLA Ops:
  6.5 0.0 copy-start
  6.5 0.0 all-gather.3.cloned.1.call-start
  6.5 0.7 all-gather.3.cloned.1.call-update
  7.3 0.0 all-gather.5.cloned.1.call-start
  7.3 0.7 all-gather.5.cloned.1.call-update
  8.0 5.6 copy.27
  13.6 0.0 copy-start.2
  13.6 5.5 copy.28
  19.1 0.0 copy-done
  19.1 0.0 copy-done.2
  19.1 5.4 convolution_multiply_fusion
  24.5 5.5 copy.29
  29.9 52.6 %all_to_all.65 = f32[128,16,512]{0,1,2:T(8,128)S(1)} all-to-all(f32[128,16,512]{0,1,2:T(8,128)} %copy.29), channel_id=1, replica_groups=mesh['seq'=16,'tensor'=8] {'seq'}, dimensions={2} | all-to-all | bytes 8388608 | tf_op jit(solution)/shard_map/all_to_all | solution.py:45
  82.6 0.0 copy-start.3
  82.6 1.3 copy.31
  83.9 0.0 copy-done.3
  83.9 11.5 %fusion.20 = f32[128,256,32]{1,0,2:T(8,128)} fusion(f32[128,256,32]{0,2,1:T(8,128)S(1)} %bitcast.75, f32[256,256]{1,0:T(8,128)S(1)} %copy-done.3), kind=kOutput, calls=%fused_computation.26 | convolution fusion | flops 3221225472 | bytes 8650752 | tf_op jit(solution)/shard_map/pa,caj->cpj/dot_general | solution.py:42
  95.4 5.5 copy.33
  100.9 7.4 all-to-all-start.1
  108.3 3.2 copy.25
  111.6 0.8 dynamic_slice.6
  112.3 0.8 dynamic_slice.7
  113.1 55.2 %all-to-all-done.1 = f32[128,256,32]{0,2,1:T(8,128)} async-done(((f32[128,256,32]{0,2,1:T(8,128)}), f32[128,256,32]{0,2,1:T(8,128)}, u32[]{:S(2)}, u32[]{:S(2)}) %all-to-all-start.1) | async-done | bytes 4194336 | tf_op jit(solution)/shard_map/all_to_all | solution.py:48
  168.3 2.7 copy.34
  171.0 2.7 fusion.19
  173.7 3.9 copy.35
  177.6 47.1 %all_to_all.66 = bf16[128,8,1024]{2,0,1:T(8,128)(2,1)S(1)} all-to-all(bf16[128,8,1024]{2,0,1:T(8,128)(2,1)} %copy.35), channel_id=1, replica_groups=mesh['seq'=16,'tensor'=8] {'tensor'}, dimensions={1} | all-to-all | bytes 4194304 | tf_op jit(solution)/shard_map/all_to_all | solution.py:55
  224.7 0.5 fusion.15
  225.2 1.9 fusion.16
  227.1 172.0 %all-gather.3.cloned.1.call-done = bf16[1024,6144]{0,1:T(8,128)(2,1)} async-done(((bf16[1024,48]{0,1:T(8,128)(2,1)}), bf16[1024,6144]{0,1:T(8,128)(2,1)}) %all-gather.3.cloned.1.call-update) | async-done | bytes 12582928 | tf_op jit(solution)/shard_map/all_gather | solution.py:57
  399.0 24.8 %fusion.48 = bf16[6144,1024]{0,1:T(8,128)(2,1)} fusion(bf16[1024,6144]{0,1:T(8,128)(2,1)} %all-gather.3.cloned.1.call-done, bf16[1024,1024]{1,0:T(8,128)(2,1)} %fusion.16), kind=kOutput, calls=%bitcast_fusion.1.clone.1 | convolution fusion | flops 12941524992 | bytes 27262976 | tf_op jit(solution)/shard_map/ch,cl->hl/dot_general | solution.py:19
  423.9 299.1 %all-gather.5.cloned.1.call-done = bf16[6144,1024]{1,0:T(8,128)(2,1)} async-done(((bf16[48,1024]{1,0:T(8,128)(2,1)}), bf16[6144,1024]{1,0:T(8,128)(2,1)}) %all-gather.5.cloned.1.call-update) | async-done | bytes 12582928 | tf_op jit(solution)/shard_map/all_gather | solution.py:58
  723.0 18.9 %fusion.14 = bf16[1024,1024]{1,0:T(8,128)(2,1)} fusion(bf16[128,8,1024]{2,0,1:T(8,128)(2,1)S(1)} %all_to_all.66, bf16[6144,1024]{1,0:T(8,128)(2,1)} %all-gather.5.cloned.1.call-done, bf16[6144,1024]{0,1:T(8,128)(2,1)} %fusion.48), kind=kOutput, calls=%fused_computation.18 | convolution fusion | flops 12888047616 | bytes 29360128 | tf_op jit(solution)/shard_map/hc,hl->cl/dot_general | solution.py:59
  741.9 0.0 copy-start.1
  741.9 33.0 %all_to_all.67 = bf16[8,128,1024]{2,1,0:T(8,128)(2,1)S(1)} all-to-all(bf16[8,128,1024]{2,1,0:T(8,128)(2,1)} %bitcast.80), channel_id=1, replica_groups=mesh['seq'=16,'tensor'=8] {'tensor'}, dimensions={0} | all-to-all | bytes 4194304 | tf_op jit(solution)/shard_map/all_to_all | solution.py:61
  774.9 1.5 copy.39
  776.4 0.0 copy-done.1
  (1 shorter events, 0.0 us)
Async XLA Ops:
  6.5 12.6 %copy-start = (bf16[512,512]{1,0:T(8,128)(2,1)S(1)}, bf16[512,512]{1,0:T(8,128)(2,1)}, u32[]{:S(2)}) copy-start(bf16[512,512]{1,0:T(8,128)(2,1)} %param.9) | copy-start | bytes 1572868
  6.5 392.5 %all-gather.3.cloned.1.call-start = ((), (), s32[]{:S(2)}) async-start(), calls=%async_computation.4 | async-start | bytes 12681216 | tf_op jit(solution)/shard_map/all_gather | solution.py:57
  7.3 715.7 %all-gather.5.cloned.1.call-start = ((), (), s32[]{:S(2)}) async-start(), calls=%async_computation.5 | async-start | bytes 12681216 | tf_op jit(solution)/shard_map/all_gather | solution.py:58
  13.6 5.5 copy-start.2
  82.6 1.3 copy-start.3
  100.9 67.4 %all-to-all-start.1 = ((f32[128,256,32]{0,2,1:T(8,128)}), f32[128,256,32]{0,2,1:T(8,128)}, u32[]{:S(2)}, u32[]{:S(2)}) async-start(f32[128,256,32]{0,2,1:T(8,128)} %copy.33), calls=%async_computation.1 | async-start | bytes 8388608 | tf_op jit(solution)/shard_map/all_to_all | solution.py:48
  741.9 34.5 %copy-start.1 = (bf16[512,512]{1,0:T(8,128)(2,1)S(1)}, bf16[512,512]{1,0:T(8,128)(2,1)}, u32[]{:S(2)}) copy-start(bf16[512,512]{1,0:T(8,128)(2,1)} %param.9) | copy-start | bytes 1572868
Sparse Core Ops, SparseCore 0:
  9.0 389.9 all-gather.2
  400.7 322.2 all-gather.4
where the time goes:
time: 789 us; the launch traced here: 783 us
  waiting for transfers between devices  528 us (67%)
  blocking collectives  133 us (17%)
  matrix products  60.6 us (8%)
  local copies, waits for them, and re-layouts  36.2 us (5%)
  between operations  13.4 us (2%)
    all_gather x1, waiting for transfers between devices, on_device(): lax.all_gather(reduce_weight, ('seq', 'tensor'), axis=0, tiled=True)  299 us
    all_gather x1, waiting for transfers between devices, on_device(): lax.all_gather(expand_weight, ('seq', 'tensor'), axis=1, tiled=True)  172 us
    all_to_all x1, waiting for transfers between devices, on_device(): lax.all_to_all(mixed_part, 'seq', split_axis=1, concat_axis=2, tiled=True)  55.2 us
    all_to_all x1, blocking collectives, on_device(): lax.all_to_all(spectrum, 'seq', split_axis=2, concat_axis=1, tiled=True)  52.6 us
    all_to_all x1, blocking collectives, on_device(): lax.all_to_all(residual_in, 'tensor', split_axis=1, concat_axis=0, tiled=...  47.1 us
    all_to_all x1, blocking collectives, on_device(): lax.all_to_all(combined, 'tensor', split_axis=0, concat_axis=1, tiled=True)  33 us
    dot_general x1, matrix products, expand(): jnp.einsum('ch,cl->hl', shard_rows, normed, preferred_element_type=jnp.fl...  24.8 us
    dot_general x1, matrix products, on_device(): jnp.einsum('hc,hl->cl', weight_full, hidden, preferred_element_type=jnp.f...  18.9 us
  transfers between devices with their start and end apart: 3, of which 3 were waited for; matrix products, arithmetic and copies ran while one was open for 10% of the time, Pallas kernels for 0%

commit v1 on v0

v1 whole, which is shorter than its diff:
```python
import functools

import jax
import jax.numpy as jnp
from jax import lax
from jax.experimental import pallas as pl
from jax.experimental.pallas import tpu as pltpu
from jax.sharding import PartitionSpec as P

MESH = pl.DeviceIdType.MESH
NC = 2
CH = 128 // NC
CP = 8 // NC
TB = 256
NT = 1024 // TB
LANES = 128
ORDERS = (("x", "y", "z"), ("y", "z", "x"), ("z", "x", "y"))
epsilon = 1e-06
f32, bf16 = jnp.float32, jnp.bfloat16


def kernel(
    act, f1, spec, f2, scale, shift, we, wr, out,
    act_v, f1_v, spec_v, f2_v, f2_b, sc_v, sh_v, sc_t, sh_t,
    we_all, wr_s, wr_t, x32, s_send, s_recv, m_send, m_recv, r_send, r_recv,
    n_all, h_buf, p_send, p_recv, o_send,
    in_sem, w_sem, own_sem, a1s, a1r, a2s, a2r, a3s, a3r, a4s, a4r, ns, nr, ps, pr,
    g1s, g1r, g2s, g2r, g3s, g3r,
):
    seq = lax.axis_index("seq")
    ten = lax.axis_index("tensor")
    core = seq % 2
    z = (seq // 2) % 4
    y_lo = seq // 8
    x = ten // 2
    y = (ten % 2) * 2 + y_lo
    pos = {"x": x, "y": y, "z": z}

    def at(axis, step):
        p = dict(pos)
        p[axis] = (p[axis] + step) % 4
        return ((p["y"] % 2) * 8 + p["z"] * 2 + core, p["x"] * 2 + p["y"] // 2)

    partner = (seq + 1 - 2 * core, ten)

    def remote(src, dst, s, r, dev):
        return pltpu.make_async_remote_copy(
            src_ref=src, dst_ref=dst, send_sem=s, recv_sem=r, device_id=dev, device_id_type=MESH
        )

    ins = [
        pltpu.make_async_copy(a, b, in_sem.at[i])
        for i, (a, b) in enumerate(
            ((act, act_v), (f1, f1_v), (spec, spec_v), (f2, f2_v), (scale, sc_v), (shift, sh_v))
        )
    ]
    wins = []
    for i, (d1, d2, d3) in enumerate(ORDERS):
        row = (pos[d3] * 16 + pos[d2] * 4 + pos[d1]) * 16
        row_s = (pos[d2] * 4 + pos[d1]) * 16
        wins.append(pltpu.make_async_copy(
            we.at[pl.ds(16 * i, 16)], we_all.at[i, pl.ds(pl.multiple_of(row, 16), 16)], w_sem.at[i, 0]))
        wins.append(pltpu.make_async_copy(
            wr.at[pl.ds(16 * i, 16)], wr_s.at[i, pl.ds(pl.multiple_of(row_s, 16), 16)], w_sem.at[i, 1]))
    for c in wins + ins:
        c.start()

    barrier = pltpu.get_barrier_semaphore()
    for r in range(1, 16):
        pl.semaphore_signal(barrier, inc=1, device_id=((seq + r) % 16, ten), device_id_type=MESH)
    for r in range(1, 8):
        pl.semaphore_signal(barrier, inc=1, device_id=(seq, (ten + r) % 8), device_id_type=MESH)
    diagonal = ((1 - y_lo) * 8 + z * 2 + core, x * 2 + 1 - ten % 2)
    pl.semaphore_signal(barrier, inc=1, device_id=diagonal, device_id_type=MESH)
    pl.semaphore_wait(barrier, 23)

    def gather_copies(stage):
        sem_s, sem_r = ((g1s, g1r), (g2s, g2r))[stage]
        copies = []
        for i, (d1, d2, d3) in enumerate(ORDERS):
            n = (16, 64)[stage]
            base = pos[d2] * 4 + (pos[d1] if stage == 0 else 0)
            row = pl.multiple_of((pos[d3] * 16 + base) * 16, n)
            row_s = pl.multiple_of(base * 16, n)
            for step in (1, 2, 3):
                dev = at((d1, d2)[stage], step)
                a = we_all.at[i, pl.ds(row, n)]
                b = wr_s.at[i, pl.ds(row_s, n)]
                copies.append(remote(a, a, sem_s.at[i, step - 1, 0], sem_r.at[i, step - 1, 0], dev))
                copies.append(remote(b, b, sem_s.at[i, step - 1, 1], sem_r.at[i, step - 1, 1], dev))
        return copies

    def block_copies(which):
        copies = []
        for i, (d1, d2, d3) in enumerate(ORDERS):
            p = pos[d3]
            if which == 0:
                for q, step in ((0, 1), (1, 3)):
                    dev = at(d3, step)
                    a = we_all.at[i, pl.ds(pl.multiple_of(p * 256, 256), 256)]
                    b = wr_t.at[i, :, pl.ds(pl.multiple_of(p * 256, 256), 256)]
                    copies.append(remote(a, a, g3s.at[i, q, 0], g3r.at[i, q, 0], dev))
                    copies.append(remote(b, b, g3s.at[i, q, 1], g3r.at[i, q, 1], dev))
            else:
                for q, source, step in ((0, 3, 1), (1, 1, 3)):
                    dev = at(d3, step)
                    o = (p + source) % 4 * 256
                    a = we_all.at[i, pl.ds(pl.multiple_of(o + 128 * q, 128), 128)]
                    b = wr_t.at[i, pl.ds(512 * q, 512), pl.ds(pl.multiple_of(o, 256), 256)]
                    copies.append(remote(a, a, g3s.at[i, 2 + q, 0], g3r.at[i, 2 + q, 0], dev))
                    copies.append(remote(b, b, g3s.at[i, 2 + q, 1], g3r.at[i, 2 + q, 1], dev))
        return copies

    for c in wins:
        c.wait()
    g1 = gather_copies(0)
    for c in g1:
        c.start()
    for c in ins:
        c.wait()

    sc_t[...] = jnp.broadcast_to(sc_v[pl.ds(ten, 1), :], (LANES, LANES)).T
    sh_t[...] = jnp.broadcast_to(sh_v[pl.ds(ten, 1), :], (LANES, LANES)).T
    f2_b[...] = f2_v[...].astype(bf16)

    def first(a, _):
        cols = pl.ds(pl.multiple_of(a * 512, 512), 512)
        value = jnp.dot(act_v[:, cols], f1_v[...], preferred_element_type=f32) * spec_v[:, cols]
        for g in range(4):
            x32[g, pl.ds(a, 128, stride=16), :] = value[:, g * LANES:(g + 1) * LANES]
        return 0

    lax.fori_loop(0, 16, first, 0)

    def a1_copy(k, r):
        to = (seq + r) % 16
        return remote(
            s_send.at[pl.ds(CH * k + CP * to, CP)],
            s_recv.at[pl.ds(CP * k, CP), pl.ds(pl.multiple_of(16 * seq, 16), 16), :],
            a1s.at[k, r], a1r.at[k, r], (to, ten))

    def a1_own(k):
        return pltpu.make_async_copy(
            s_send.at[pl.ds(CH * k + CP * seq, CP)],
            s_recv.at[pl.ds(CP * k, CP), pl.ds(pl.multiple_of(16 * seq, 16), 16), :],
            own_sem.at[0, k])

    def a2_copy(k, r):
        to = (seq + r) % 16
        return remote(
            m_send.at[pl.ds(CP * k, CP), pl.ds(pl.multiple_of(16 * to, 16), 16), :],
            m_recv.at[pl.ds(CH * k + CP * seq, CP)],
            a2s.at[k, r], a2r.at[k, r], (to, ten))

    def a2_own(k):
        return pltpu.make_async_copy(
            m_send.at[pl.ds(CP * k, CP), pl.ds(pl.multiple_of(16 * seq, 16), 16), :],
            m_recv.at[pl.ds(CH * k + CP * seq, CP)],
            own_sem.at[1, k])

    def a3_refs(k, to):
        src = r_send.at[pl.ds(CH * k, CH), pl.ds(pl.multiple_of(to * 1024, 1024), 1024)]
        dst = r_recv.at[pl.ds(pl.multiple_of(128 * ten + CH * k, CH), CH)]
        return src, dst

    def a3_copy(k, r):
        to = (ten + r) % 8
        src, dst = a3_refs(k, to)
        return remote(src, dst, a3s.at[k, r], a3r.at[k, r], (seq, to))

    def a3_own(k):
        src, dst = a3_refs(k, ten)
        return pltpu.make_async_copy(src, dst, own_sem.at[2, k])

    def a4_refs(b, to):
        src = o_send.at[b, pl.ds(pl.multiple_of(to * 128, 128), 128)]
        dst = out.at[:, pl.ds(pl.multiple_of(ten * 1024 + b * TB, TB), TB)]
        return src, dst

    def a4_copy(b, r):
        to = (ten + r) % 8
        src, dst = a4_refs(b, to)
        return remote(src, dst, a4s.at[b, r], a4r.at[b, r], (seq, to))

    def a4_own(b):
        src, dst = a4_refs(b, ten)
        return pltpu.make_async_copy(src, dst, a4s.at[b, 0])

    def loop(lo, hi, body):
        def step(i, _):
            body(i)
            return 0
        lax.fori_loop(lo, hi, step, 0)

    for k in range(NC):
        def cast(n, k=k):
            c = CH * k + 8 * n
            for g in range(4):
                rows = x32[g, pl.ds(pl.multiple_of(c * 16, 128), 128), :]
                s_send[pl.ds(c, 8), :, g * LANES:(g + 1) * LANES] = rows.astype(bf16).reshape(8, 16, LANES)
        loop(0, CH // 8, cast)
        a1_own(k).start()
        loop(1, 16, lambda r, k=k: a1_copy(k, r).start())

    for c in g1:
        c.wait_recv()
    g2 = gather_copies(1)
    for c in g2:
        c.start()
    for c in g2:
        c.wait_recv()
    for i, (d1, d2, d3) in enumerate(ORDERS):
        col = pl.ds(pl.multiple_of(pos[d3] * 256, 256), 256)
        def turn(n, i=i, col=col):
            c = pl.multiple_of(n * 256, 256)
            wr_t[i, pl.ds(c, 256), col] = wr_s[i, :, pl.ds(c, 256)].astype(f32).T.astype(bf16)
        loop(0, 4, turn)
    g3 = block_copies(0)
    for c in g3:
        c.start()

    for k in range(NC):
        a1_own(k).wait()
        loop(1, 16, lambda r, k=k: a1_copy(k, r).wait_recv())
        def mix(n, k=k):
            c = CP * k + n
            m_send[c] = jnp.dot(f2_b[...], s_recv[c], preferred_element_type=f32).astype(bf16)
        loop(0, CP, mix)
        a2_own(k).start()
        loop(1, 16, lambda r, k=k: a2_copy(k, r).start())

    for c in g3:
        c.wait_recv()
    g4 = block_copies(1)
    for c in g4:
        c.start()

    for k in range(NC):
        a2_own(k).wait()
        loop(1, 16, lambda r, k=k: a2_copy(k, r).wait_recv())
        def widen(n, k=k):
            c = CH * k + 8 * n
            rows = m_recv[pl.ds(c, 8)].astype(f32).reshape(128, 512)
            for g in range(4):
                x32[g, pl.ds(pl.multiple_of(c * 16, 128), 128), :] = rows[:, g * LANES:(g + 1) * LANES]
        loop(0, CH // 8, widen)
        chans = pl.ds(CH * k, CH)
        def gate(p, k=k, chans=chans):
            for g in range(4):
                cols = pl.ds(pl.multiple_of(p * 512 + g * LANES, LANES), LANES)
                mixed = x32[g, pl.ds(CH * k * 16 + p, CH, stride=16), :]
                value = act_v[chans, cols].astype(f32)
                gating = jax.nn.sigmoid(value * sc_t[chans, :] + sh_t[chans, :])
                r_send[chans, cols] = (value + gating * mixed).astype(bf16)
        loop(0, 16, gate)
        a3_own(k).start()
        loop(1, 8, lambda r, k=k: a3_copy(k, r).start())

    for k in range(NC):
        a3_own(k).wait()
        loop(1, 8, lambda r, k=k: a3_copy(k, r).wait_recv())

    def norm_copy(b):
        cols = pl.ds(pl.multiple_of(b * TB, TB), TB)
        return remote(n_all.at[0, :, cols], n_all.at[1, :, cols], ns.at[b], nr.at[b], partner)

    def normalize(b):
        cols = pl.ds(pl.multiple_of(b * TB, TB), TB)
        def square(n, total):
            v = r_recv[pl.ds(pl.multiple_of(n * 64, 64), 64), cols].astype(f32)
            return total + jnp.sum((v * v).reshape(8, 8, TB), axis=0)
        total = lax.fori_loop(0, 16, square, jnp.zeros((8, TB), f32))
        factor = lax.rsqrt(jnp.sum(total, axis=0, keepdims=True) * (1.0 / 1024) + epsilon)
        def write(n):
            rows = pl.ds(pl.multiple_of(n * 64, 64), 64)
            n_all[0, rows, cols] = (r_recv[rows, cols].astype(f32) * factor).astype(bf16)
        loop(0, 16, write)
        norm_copy(b).start()

    loop(0, NT, normalize)

    for c in g4:
        c.wait_recv()

    def mlp(which, cols):
        tokens = n_all[which, :, cols]
        for i in range(3):
            product = jnp.dot(we_all[i], tokens, preferred_element_type=f32)
            h_buf[i] = jax.nn.gelu(product).astype(bf16)
        total = jnp.dot(wr_t[0], h_buf[0], preferred_element_type=f32)
        for i in (1, 2):
            total += jnp.dot(wr_t[i], h_buf[i], preferred_element_type=f32)
        return total

    def part_copy(b):
        return remote(p_send.at[b], p_recv.at[b], ps.at[b], pr.at[b], partner)

    def theirs(b):
        norm_copy(b).wait_recv()
        cols = pl.ds(pl.multiple_of(b * TB, TB), TB)
        p_send[b] = mlp(1, cols).astype(bf16)
        part_copy(b).start()

    loop(0, NT, theirs)

    def ours(b):
        cols = pl.ds(pl.multiple_of(b * TB, TB), TB)
        total = mlp(0, cols)
        part_copy(b).wait_recv()
        o_send[b] = (r_recv[:, cols].astype(f32) + (total + p_recv[b].astype(f32))).astype(bf16)
        a4_own(b).start()
        loop(1, 8, lambda r: a4_copy(b, r).start())

    loop(0, NT, ours)

    def drain(b):
        a4_own(b).wait()
        loop(1, 8, lambda r: a4_copy(b, r).wait_recv())
        loop(1, 8, lambda r: a4_copy(b, r).wait_send())
        norm_copy(b).wait_send()
        part_copy(b).wait_send()
    loop(0, NT, drain)
    for c in g1 + g2 + g3 + g4:
        c.wait_send()
    for k in range(NC):
        loop(1, 16, lambda r, k=k: a1_copy(k, r).wait_send())
        loop(1, 16, lambda r, k=k: a2_copy(k, r).wait_send())
        loop(1, 8, lambda r, k=k: a3_copy(k, r).wait_send())


def on_device(act, f1, spec, f2, scale, shift, we, wr):
    vmem, dma = pltpu.VMEM, pltpu.SemaphoreType.DMA
    scratch = [
        vmem((128, 8192), bf16), vmem((512, 512), bf16), vmem((128, 8192), f32), vmem((256, 256), f32),
        vmem((256, 256), bf16), vmem((8, 128), f32), vmem((8, 128), f32),
        vmem((128, 128), f32), vmem((128, 128), f32),
        vmem((3, 1024, 1024), bf16), vmem((3, 256, 1024), bf16), vmem((3, 1024, 1024), bf16),
        vmem((4, 2048, 128), f32),
        vmem((128, 16, 512), bf16), vmem((8, 256, 512), bf16),
        vmem((8, 256, 512), bf16), vmem((128, 16, 512), bf16),
        vmem((128, 8192), bf16), vmem((1024, 1024), bf16),
        vmem((2, 1024, 1024), bf16), vmem((3, 1024, TB), bf16),
        vmem((NT, 1024, TB), bf16), vmem((NT, 1024, TB), bf16), vmem((NT, 1024, TB), bf16),
        dma((6,)), dma((3, 2)), dma((3, NC)),
        dma((NC, 16)), dma((NC, 16)), dma((NC, 16)), dma((NC, 16)),
        dma((NC, 8)), dma((NC, 8)), dma((NT, 8)), dma((NT, 8)),
        dma((NT,)), dma((NT,)), dma((NT,)), dma((NT,)),
        dma((3, 3, 2)), dma((3, 3, 2)), dma((3, 3, 2)), dma((3, 3, 2)), dma((3, 4, 2)), dma((3, 4, 2)),
    ]
    return pl.pallas_call(
        kernel,
        out_shape=jax.ShapeDtypeStruct((128, 8192), bf16),
        in_specs=[pl.BlockSpec(memory_space=pl.ANY)] * 8,
        out_specs=pl.BlockSpec(memory_space=pl.ANY),
        scratch_shapes=scratch,
        compiler_params=pltpu.CompilerParams(
            collective_id=0, has_side_effects=True, vmem_limit_bytes=67_043_328),
        name="mixer",
    )(act, f1, spec, f2, scale.reshape(8, 128), shift.reshape(8, 128), we.T, wr)


def solution(mesh):
    return jax.shard_map(
        on_device,
        mesh=mesh,
        in_specs=(
            P("tensor", "seq"),
            P(),
            P("tensor", "seq"),
            P(),
            P(),
            P(),
            P(None, ("seq", "tensor")),
            P(("seq", "tensor"), None),
        ),
        out_specs=P("tensor", "seq"),
        check_vma=False,
    )
```

time: 789 us -> 201 us (0.25)
  the two profiles are of different devices: /device:TPU:108 before, /device:TPU:17 now
where the time goes in v1:
time: 201 us; the launch traced here: 200 us
  Pallas kernels  197 us (98%)
  local copies, waits for them, and re-layouts  3.1 us (2%)
    pallas_call x1, Pallas kernels, on_device(): pl.pallas_call(kernel, out_shape=jax.ShapeDtypeStruct((128, 8192), bf16),...  197 us

profile of v1, /device:TPU:17, one launch (start us, length us, event | category | flops | bytes accessed | tf_op | source)
XLA Modules:
  0.0 200.4 jit_solution(4457156490332321745)
XLA Ops:
  0.0 197.3 %mixer.1 = bf16[128,8192]{1,0:T(8,128)(2,1)} custom-call(bf16[128,8192]{1,0:T(8,128)(2,1)} %act.1, bf16[512,512]{1,0:T(8,128)(2,1)} %f1.1, f32[128,8192]{1,0:T(8,128)} %spec.1, f32[256,256]{1,0:T(8,128)} %f2.1, f32[8,128]{1,0:T(8,128)} %bitcast.4, f32[8,128]{1,0:T(8,128)} %bitcast.5, bf16[48,1024]{1,0:T(8,128)(2,1)} %bitcast.3, bf16[48,1024]{1,0:T(8,128)(2,1)} %wr.1), custom_call_target="tpu_custom_call" | custom-call | tf_op jit(solution)/shard_map/mixer/pallas_call | solution.py:350
  197.3 3.1 %copy.10 = bf16[128,8192]{1,0:T(8,128)(2,1)} copy(bf16[128,8192]{1,0:T(8,128)(2,1)} %mixer.1) | data formatting | bytes 4194304

commit v2 on v1

v2 whole, which is shorter than its diff:
```python
import functools

import jax
import jax.numpy as jnp
from jax import lax
from jax.experimental import pallas as pl
from jax.experimental.pallas import tpu as pltpu
from jax.sharding import PartitionSpec as P

MESH = pl.DeviceIdType.MESH
NK = 2
W = 512 // NK
TB = 256
NT = 4
LANES = 128
ORDERS = (("y", "z", "x"), ("y", "x", "z"), ("y", "z", "x"))
TURNED = (True, False, True)
epsilon = 1e-06
f32, bf16 = jnp.float32, jnp.bfloat16


def kernel(
    act, f1, spec, f2, scale, shift, we, wr, out,
    act_v, f1_v, spec_v, f2_v, f2_b, sc_v, sh_v, sc_t, sh_t,
    we_all, wr_s, wr_t, x32, s_send, s_recv, m_send, m_recv, r_send, r_recv,
    n_all, acc, h_buf, p_send, p_recv, o_send,
    in_sem, w_sem, own_sem, a1s, a1r, a2s, a2r, a3s, a3r, a4s, a4r, ns, nr, ps, pr,
    g1s, g1r, g2s, g2r, g3s, g3r,
):
    seq = lax.axis_index("seq")
    ten = lax.axis_index("tensor")
    core = seq % 2
    z = (seq // 2) % 4
    y_lo = seq // 8
    x = ten // 2
    y = (ten % 2) * 2 + y_lo
    pos = {"x": x, "y": y, "z": z}

    def at(axis, step):
        p = dict(pos)
        p[axis] = (p[axis] + step) % 4
        return ((p["y"] % 2) * 8 + p["z"] * 2 + core, p["x"] * 2 + p["y"] // 2)

    partner = (seq + 1 - 2 * core, ten)

    def remote(src, dst, s, r, dev):
        return pltpu.make_async_remote_copy(
            src_ref=src, dst_ref=dst, send_sem=s, recv_sem=r, device_id=dev, device_id_type=MESH
        )

    ins = [
        pltpu.make_async_copy(a, b, in_sem.at[i])
        for i, (a, b) in enumerate(
            ((act, act_v), (f1, f1_v), (spec, spec_v), (f2, f2_v), (scale, sc_v), (shift, sh_v))
        )
    ]
    wins = []
    for i, (d1, d2, d3) in enumerate(ORDERS):
        row = (pos[d3] * 16 + pos[d2] * 4 + pos[d1]) * 16
        wins.append(pltpu.make_async_copy(
            we.at[pl.ds(16 * i, 16)], we_all.at[i, pl.ds(pl.multiple_of(row, 16), 16)], w_sem.at[i, 0]))
        wins.append(pltpu.make_async_copy(
            wr.at[pl.ds(16 * i, 16)], wr_s.at[i, pos[d2], pos[d1]], w_sem.at[i, 1]))
    for c in wins + ins:
        c.start()

    barrier = pltpu.get_barrier_semaphore()
    for r in range(1, 16):
        pl.semaphore_signal(barrier, inc=1, device_id=((seq + r) % 16, ten), device_id_type=MESH)
    for r in range(1, 8):
        pl.semaphore_signal(barrier, inc=1, device_id=(seq, (ten + r) % 8), device_id_type=MESH)
    diagonal = ((1 - y_lo) * 8 + z * 2 + core, x * 2 + 1 - ten % 2)
    pl.semaphore_signal(barrier, inc=1, device_id=diagonal, device_id_type=MESH)

    def gather_copies(stage, i):
        sem_s, sem_r = ((g1s, g1r), (g2s, g2r))[stage]
        d1, d2, d3 = ORDERS[i]
        n = (16, 64)[stage]
        base = pos[d2] * 4 + (pos[d1] if stage == 0 else 0)
        a = we_all.at[i, pl.ds(pl.multiple_of((pos[d3] * 16 + base) * 16, n), n)]
        if stage == 0:
            b = wr_s.at[i, pos[d2], pos[d1]]
        elif TURNED[i]:
            b = wr_s.at[i, :, pos[d1]]
        else:
            b = wr_s.at[i, pos[d2]]
        copies = []
        for step in (1, 3, 2):
            dev = at((d1, d2)[stage], step)
            copies.append(remote(a, a, sem_s.at[i, step - 1, 0], sem_r.at[i, step - 1, 0], dev))
            dev = at((d1, d2)[1 - stage if TURNED[i] else stage], step)
            copies.append(remote(b, b, sem_s.at[i, step - 1, 1], sem_r.at[i, step - 1, 1], dev))
        return copies

    def block_copies(which, i):
        d3 = ORDERS[i][2]
        p = pos[d3]
        copies = []
        if which == 0:
            a = we_all.at[i, pl.ds(pl.multiple_of(p * 256, 256), 256)]
            b = wr_t.at[i, :, pl.ds(pl.multiple_of(p * 256, 256), 256)]
            for q, step in ((0, 1), (1, 3)):
                dev = at(d3, step)
                copies.append(remote(a, a, g3s.at[i, q, 0], g3r.at[i, q, 0], dev))
                copies.append(remote(b, b, g3s.at[i, q, 1], g3r.at[i, q, 1], dev))
        else:
            for q, source, step in ((0, 3, 1), (1, 1, 3)):
                dev = at(d3, step)
                o = (p + source) % 4 * 256
                a = we_all.at[i, pl.ds(pl.multiple_of(o + 128 * q, 128), 128)]
                b = wr_t.at[i, pl.ds(512 * q, 512), pl.ds(pl.multiple_of(o, 256), 256)]
                copies.append(remote(a, a, g3s.at[i, 2 + q, 0], g3r.at[i, 2 + q, 0], dev))
                copies.append(remote(b, b, g3s.at[i, 2 + q, 1], g3r.at[i, 2 + q, 1], dev))
        return copies

    g1 = [gather_copies(0, i) for i in range(3)]
    g2 = [gather_copies(1, i) for i in range(3)]
    g3 = [block_copies(0, i) for i in range(3)]
    g4 = [block_copies(1, i) for i in range(3)]

    def start(copies):
        for c in copies:
            c.start()

    def arrive(copies):
        for c in copies:
            c.wait_recv()

    def loop(lo, hi, body, unroll=1):
        def step(i, _):
            body(i)
            return 0
        lax.fori_loop(lo, hi, step, 0, unroll=unroll)

    def turn(i):
        col = pl.ds(pl.multiple_of(pos[ORDERS[i][2]] * 256, 256), 256)
        def piece(n):
            c = pl.multiple_of(n * 256, 256)
            rows = wr_s[i, :, :, :, pl.ds(c, 256)].astype(f32).reshape(256, 256)
            wr_t[i, pl.ds(c, 256), col] = rows.T.astype(bf16)
        loop(0, 4, piece)

    def a1_refs(k, to):
        src = s_send.at[k, pl.ds(8 * to, 8)]
        dst = s_recv.at[k, :, pl.ds(pl.multiple_of(16 * seq, 16), 16), :]
        return src, dst

    def a1_copy(k, r):
        to = (seq + r) % 16
        src, dst = a1_refs(k, to)
        return remote(src, dst, a1s.at[k, r], a1r.at[k, r], (to, ten))

    def a1_own(k):
        src, dst = a1_refs(k, seq)
        return pltpu.make_async_copy(src, dst, own_sem.at[0, k])

    def a2_refs(k, to):
        src = m_send.at[k, :, pl.ds(pl.multiple_of(16 * to, 16), 16), :]
        dst = m_recv.at[k, pl.ds(8 * seq, 8)]
        return src, dst

    def a2_copy(k, r):
        to = (seq + r) % 16
        src, dst = a2_refs(k, to)
        return remote(src, dst, a2s.at[k, r], a2r.at[k, r], (to, ten))

    def a2_own(k):
        src, dst = a2_refs(k, seq)
        return pltpu.make_async_copy(src, dst, own_sem.at[1, k])

    def a3_refs(k, to):
        src = r_send.at[k, to]
        dst = r_recv.at[pl.ds(2 * k, 2), pl.ds(pl.multiple_of(128 * ten, 128), 128)]
        return src, dst

    def a3_copy(k, r):
        to = (ten + r) % 8
        src, dst = a3_refs(k, to)
        return remote(src, dst, a3s.at[k, r], a3r.at[k, r], (seq, to))

    def a3_own(k):
        src, dst = a3_refs(k, ten)
        return pltpu.make_async_copy(src, dst, own_sem.at[2, k])

    def a4_refs(b, to):
        src = o_send.at[b, pl.ds(pl.multiple_of(to * 128, 128), 128)]
        dst = out.at[:, pl.ds(pl.multiple_of(ten * 1024 + (b % 2) * 512 + (b // 2) * TB, TB), TB)]
        return src, dst

    def a4_copy(b, r):
        to = (ten + r) % 8
        src, dst = a4_refs(b, to)
        return remote(src, dst, a4s.at[b, r], a4r.at[b, r], (seq, to))

    def a4_own(b):
        src, dst = a4_refs(b, ten)
        return pltpu.make_async_copy(src, dst, a4s.at[b, 0])

    for c in ins:
        c.wait()

    def first(k):
        def block(a):
            value = jnp.dot(
                act_v[:, pl.ds(pl.multiple_of(a * 512, 512), 512)], f1_v[:, W * k:W * (k + 1)],
                preferred_element_type=f32)
            value = value * spec_v[:, pl.ds(pl.multiple_of(a * 512 + W * k, W), W)]
            for g in range(W // LANES):
                x32[g, pl.ds(a, 128, stride=16), :] = value[:, g * LANES:(g + 1) * LANES]
        loop(0, 16, block, 4)

    def send_first(k):
        def cast(n):
            c = 8 * n
            for g in range(W // LANES):
                rows = x32[g, pl.ds(pl.multiple_of(c * 16, 128), 128), :]
                s_send[k, pl.ds(c, 8), :, g * LANES:(g + 1) * LANES] = rows.astype(bf16).reshape(8, 16, LANES)
        loop(0, 16, cast)
        a1_own(k).start()
        loop(1, 16, lambda r: a1_copy(k, r).start())

    first(0)
    pl.semaphore_wait(barrier, 23)
    for c in wins:
        c.wait()
    for i in range(3):
        start(g1[i])
    sc_t[...] = jnp.broadcast_to(sc_v[pl.ds(ten, 1), :], (LANES, LANES)).T
    sh_t[...] = jnp.broadcast_to(sh_v[pl.ds(ten, 1), :], (LANES, LANES)).T
    f2_b[...] = f2_v[...].astype(bf16)

    send_first(0)
    first(1)
    for i in range(3):
        arrive(g1[i])
        start(g2[i])

    def mixing(k):
        a1_own(k).wait()
        loop(1, 16, lambda r: a1_copy(k, r).wait_recv())
        if k == 0:
            send_first(1)
        def mix(c):
            m_send[k, c] = jnp.dot(f2_b[...], s_recv[k, c], preferred_element_type=f32).astype(bf16)
        loop(0, 8, mix)
        a2_own(k).start()
        loop(1, 16, lambda r: a2_copy(k, r).start())

    mixing(0)
    arrive(g2[0])
    turn(0)
    start(g3[0])
    mixing(1)
    for i in (1, 2):
        arrive(g2[i])
        turn(i)
        start(g3[i])

    def gating(k):
        a2_own(k).wait()
        loop(1, 16, lambda r: a2_copy(k, r).wait_recv())
        def widen(n):
            c = 8 * n
            rows = m_recv[k, pl.ds(c, 8)].astype(f32).reshape(128, W)
            for g in range(W // LANES):
                x32[g, pl.ds(pl.multiple_of(c * 16, 128), 128), :] = rows[:, g * LANES:(g + 1) * LANES]
        loop(0, 16, widen)
        def gate(p):
            for g in range(W // LANES):
                mixed = x32[g, pl.ds(p, 128, stride=16), :]
                cols = pl.ds(pl.multiple_of(p * 512 + W * k + g * LANES, LANES), LANES)
                value = act_v[:, cols].astype(f32)
                sig = jax.nn.sigmoid(value * sc_t[...] + sh_t[...])
                r_send[k, p // 2, p % 2, :, g * LANES:(g + 1) * LANES] = (value + sig * mixed).astype(bf16)
        loop(0, 16, gate)
        a3_own(k).start()
        loop(1, 8, lambda r: a3_copy(k, r).start())

    gating(0)
    arrive(g3[0])
    start(g4[0])
    gating(1)

    def norm_copy(b):
        return remote(n_all.at[0, b], n_all.at[1, b], ns.at[b], nr.at[b], partner)

    def normalize(b):
        def square(n, total):
            v = r_recv[b, pl.ds(pl.multiple_of(n * 64, 64), 64), :].astype(f32)
            return total + jnp.sum((v * v).reshape(8, 8, TB), axis=0)
        total = lax.fori_loop(0, 16, square, jnp.zeros((8, TB), f32))
        factor = lax.rsqrt(jnp.sum(total, axis=0, keepdims=True) * (1.0 / 1024) + epsilon)
        def write(n):
            rows = pl.ds(pl.multiple_of(n * 64, 64), 64)
            n_all[0, b, rows, :] = (r_recv[b, rows, :].astype(f32) * factor).astype(bf16)
        loop(0, 16, write)
        norm_copy(b).start()

    def mlp(i, blocks):
        for q, (which, b) in enumerate(blocks):
            product = jnp.dot(we_all[i], n_all[which, b], preferred_element_type=f32)
            h_buf[q] = jax.nn.gelu(product).astype(bf16)
        return [jnp.dot(wr_t[i], h_buf[q], preferred_element_type=f32) for q in range(2)]

    def part_copy(b):
        return remote(p_send.at[b], p_recv.at[b], ps.at[b], pr.at[b], partner)

    def opening(which, n):
        acc[which, 2 * n], acc[which, 2 * n + 1] = mlp(0, ((which, 2 * n), (which, 2 * n + 1)))

    def middle(b):
        part, total = mlp(1, ((1, b), (0, b)))
        acc[1, b] += part
        acc[0, b] += total

    def last(b):
        part, total = mlp(2, ((1, b), (0, b)))
        p_send[b] = (acc[1, b] + part).astype(bf16)
        part_copy(b).start()
        acc[0, b] += total

    def finish(b):
        part_copy(b).wait_recv()
        o_send[b] = (r_recv[b].astype(f32) + (acc[0, b] + p_recv[b].astype(f32))).astype(bf16)
        a4_own(b).start()
        loop(1, 8, lambda r: a4_copy(b, r).start())

    def settle(k):
        a3_own(k).wait()
        loop(1, 8, lambda r: a3_copy(k, r).wait_recv())
        loop(2 * k, 2 * k + 2, normalize)

    settle(0)
    arrive(g3[1])
    start(g4[1])
    arrive(g4[0])
    loop(0, 1, lambda n: opening(0, n))
    loop(0, 2, lambda b: norm_copy(b).wait_recv())
    loop(0, 1, lambda n: opening(1, n))
    arrive(g3[2])
    start(g4[2])
    settle(1)
    loop(1, 2, lambda n: opening(0, n))
    loop(2, 4, lambda b: norm_copy(b).wait_recv())
    loop(1, 2, lambda n: opening(1, n))
    arrive(g4[1])
    loop(0, 2, middle)
    arrive(g4[2])
    last(0)
    last(1)
    finish(0)
    def tail(b):
        middle(b)
        last(b)
        finish(b - 1)
    loop(2, NT, tail)
    finish(NT - 1)

    def drain(b):
        a4_own(b).wait()
        loop(1, 8, lambda r: a4_copy(b, r).wait_recv())
        loop(1, 8, lambda r: a4_copy(b, r).wait_send())
        norm_copy(b).wait_send()
        part_copy(b).wait_send()
    loop(0, NT, drain)
    for i in range(3):
        for c in g1[i] + g2[i] + g3[i] + g4[i]:
            c.wait_send()
    for k in range(NK):
        loop(1, 16, lambda r, k=k: a1_copy(k, r).wait_send())
        loop(1, 16, lambda r, k=k: a2_copy(k, r).wait_send())
        loop(1, 8, lambda r, k=k: a3_copy(k, r).wait_send())


def on_device(act, f1, spec, f2, scale, shift, we, wr):
    vmem, dma = pltpu.VMEM, pltpu.SemaphoreType.DMA
    scratch = [
        vmem((128, 8192), bf16), vmem((512, 512), bf16), vmem((128, 8192), f32), vmem((256, 256), f32),
        vmem((256, 256), bf16), vmem((8, 128), f32), vmem((8, 128), f32),
        vmem((128, 128), f32), vmem((128, 128), f32),
        vmem((3, 1024, 1024), bf16), vmem((3, 4, 4, 16, 1024), bf16), vmem((3, 1024, 1024), bf16),
        vmem((W // 128, 2048, 128), f32),
        vmem((NK, 128, 16, W), bf16), vmem((NK, 8, 256, W), bf16),
        vmem((NK, 8, 256, W), bf16), vmem((NK, 128, 16, W), bf16),
        vmem((NK, 8, 2, 128, W), bf16), vmem((NT, 1024, TB), bf16),
        vmem((2, NT, 1024, TB), bf16), vmem((2, NT, 1024, TB), f32), vmem((2, 1024, TB), bf16),
        vmem((NT, 1024, TB), bf16), vmem((NT, 1024, TB), bf16), vmem((NT, 1024, TB), bf16),
        dma((6,)), dma((3, 2)), dma((3, NK)),
        dma((NK, 16)), dma((NK, 16)), dma((NK, 16)), dma((NK, 16)),
        dma((NK, 8)), dma((NK, 8)), dma((NT, 8)), dma((NT, 8)),
        dma((NT,)), dma((NT,)), dma((NT,)), dma((NT,)),
        dma((3, 3, 2)), dma((3, 3, 2)), dma((3, 3, 2)), dma((3, 3, 2)), dma((3, 4, 2)), dma((3, 4, 2)),
    ]
    return pl.pallas_call(
        kernel,
        out_shape=jax.ShapeDtypeStruct((128, 8192), bf16),
        in_specs=[pl.BlockSpec(memory_space=pl.ANY)] * 8,
        out_specs=pl.BlockSpec(memory_space=pl.ANY),
        scratch_shapes=scratch,
        compiler_params=pltpu.CompilerParams(
            collective_id=0, has_side_effects=True, vmem_limit_bytes=67_043_328),
        name="mixer",
    )(act, f1, spec, f2, scale.reshape(8, 128), shift.reshape(8, 128), we.T, wr)


def solution(mesh):
    return jax.shard_map(
        on_device,
        mesh=mesh,
        in_specs=(
            P("tensor", "seq"),
            P(),
            P("tensor", "seq"),
            P(),
            P(),
            P(),
            P(None, ("seq", "tensor")),
            P(("seq", "tensor"), None),
        ),
        out_specs=P("tensor", "seq"),
        check_vma=False,
    )
```

time: 201 us -> 169 us (0.84)
  the two profiles are of different devices: /device:TPU:17 before, /device:TPU:108 now
where the time goes in v2:
time: 169 us; the launch traced here: 166 us
  Pallas kernels  163 us (96%)
  local copies, waits for them, and re-layouts  3.1 us (2%)
    pallas_call x1, Pallas kernels, on_device(): pl.pallas_call(kernel, out_shape=jax.ShapeDtypeStruct((128, 8192), bf16),...  163 us

profile of v2, /device:TPU:108, one launch (start us, length us, event | category | flops | bytes accessed | tf_op | source)
XLA Modules:
  0.0 166.3 jit_solution(8472700404055965440)
XLA Ops:
  0.0 163.2 %mixer.1 = bf16[128,8192]{1,0:T(8,128)(2,1)} custom-call(bf16[128,8192]{1,0:T(8,128)(2,1)} %act.1, bf16[512,512]{1,0:T(8,128)(2,1)} %f1.1, f32[128,8192]{1,0:T(8,128)} %spec.1, f32[256,256]{1,0:T(8,128)} %f2.1, f32[8,128]{1,0:T(8,128)} %bitcast.4, f32[8,128]{1,0:T(8,128)} %bitcast.5, bf16[48,1024]{1,0:T(8,128)(2,1)} %bitcast.3, bf16[48,1024]{1,0:T(8,128)(2,1)} %wr.1), custom_call_target="tpu_custom_call" | custom-call | tf_op jit(solution)/shard_map/mixer/pallas_call | solution.py:394
  163.2 3.1 %copy.10 = bf16[128,8192]{1,0:T(8,128)(2,1)} copy(bf16[128,8192]{1,0:T(8,128)(2,1)} %mixer.1) | data formatting | bytes 4194304

commit v3 on v2

--- a/solution.py
+++ b/solution.py
@@ -14,7 +14,8 @@
 NT = 4
 LANES = 128
 ORDERS = (("y", "z", "x"), ("y", "x", "z"), ("y", "z", "x"))
-TURNED = (True, False, True)
+WE_PATHS = (("y", "z", "x"), ("y", "x", "z"), ("z", "x", "y"))
+WR_PATHS = (("z", "y", "x"), ("y", "x", "z"), ("y", "z", "x"))
 epsilon = 1e-06
 f32, bf16 = jnp.float32, jnp.bfloat16
 
@@ -56,9 +57,8 @@
     ]
     wins = []
     for i, (d1, d2, d3) in enumerate(ORDERS):
-        row = (pos[d3] * 16 + pos[d2] * 4 + pos[d1]) * 16
         wins.append(pltpu.make_async_copy(
-            we.at[pl.ds(16 * i, 16)], we_all.at[i, pl.ds(pl.multiple_of(row, 16), 16)], w_sem.at[i, 0]))
+            we.at[pl.ds(16 * i, 16)], we_all.at[i, pos[d3], pos[d2], pos[d1]], w_sem.at[i, 0]))
         wins.append(pltpu.make_async_copy(
             wr.at[pl.ds(16 * i, 16)], wr_s.at[i, pos[d2], pos[d1]], w_sem.at[i, 1]))
     for c in wins + ins:
@@ -75,42 +75,44 @@
     def gather_copies(stage, i):
         sem_s, sem_r = ((g1s, g1r), (g2s, g2r))[stage]
         d1, d2, d3 = ORDERS[i]
-        n = (16, 64)[stage]
-        base = pos[d2] * 4 + (pos[d1] if stage == 0 else 0)
-        a = we_all.at[i, pl.ds(pl.multiple_of((pos[d3] * 16 + base) * 16, n), n)]
-        if stage == 0:
-            b = wr_s.at[i, pos[d2], pos[d1]]
-        elif TURNED[i]:
-            b = wr_s.at[i, :, pos[d1]]
-        else:
-            b = wr_s.at[i, pos[d2]]
+        done = WE_PATHS[i][:stage]
+        a = we_all.at[(i,) + tuple(slice(None) if d in done else pos[d] for d in (d3, d2, d1))]
+        done = WR_PATHS[i][:stage]
+        b = wr_s.at[(i,) + tuple(slice(None) if d in done else pos[d] for d in (d2, d1))]
         copies = []
         for step in (1, 3, 2):
-            dev = at((d1, d2)[stage], step)
+            dev = at(WE_PATHS[i][stage], step)
             copies.append(remote(a, a, sem_s.at[i, step - 1, 0], sem_r.at[i, step - 1, 0], dev))
-            dev = at((d1, d2)[1 - stage if TURNED[i] else stage], step)
+            dev = at(WR_PATHS[i][stage], step)
             copies.append(remote(b, b, sem_s.at[i, step - 1, 1], sem_r.at[i, step - 1, 1], dev))
         return copies
 
+    def we_block(i, p, half=None):
+        index, cut = [i], half is None
+        for d in ORDERS[i][::-1]:
+            if d == WE_PATHS[i][2]:
+                index.append(p)
+            elif cut:
+                index.append(slice(None))
+            else:
+                index.append(pl.ds(2 * half, 2))
+                cut = True
+        return we_all.at[tuple(index)]
+
     def block_copies(which, i):
-        d3 = ORDERS[i][2]
-        p = pos[d3]
+        axis_a, axis_b = WE_PATHS[i][2], WR_PATHS[i][2]
         copies = []
-        if which == 0:
-            a = we_all.at[i, pl.ds(pl.multiple_of(p * 256, 256), 256)]
-            b = wr_t.at[i, :, pl.ds(pl.multiple_of(p * 256, 256), 256)]
-            for q, step in ((0, 1), (1, 3)):
-                dev = at(d3, step)
-                copies.append(remote(a, a, g3s.at[i, q, 0], g3r.at[i, q, 0], dev))
-                copies.append(remote(b, b, g3s.at[i, q, 1], g3r.at[i, q, 1], dev))
-        else:
-            for q, source, step in ((0, 3, 1), (1, 1, 3)):
-                dev = at(d3, step)
-                o = (p + source) % 4 * 256
-                a = we_all.at[i, pl.ds(pl.multiple_of(o + 128 * q, 128), 128)]
+        for q, source, step in ((0, 3, 1), (1, 1, 3)):
+            if which == 0:
+                a = we_block(i, pos[axis_a])
+                b = wr_t.at[i, :, pl.ds(pl.multiple_of(pos[axis_b] * 256, 256), 256)]
+            else:
+                a = we_block(i, (pos[axis_a] + source) % 4, q)
+                o = (pos[axis_b] + source) % 4 * 256
                 b = wr_t.at[i, pl.ds(512 * q, 512), pl.ds(pl.multiple_of(o, 256), 256)]
-                copies.append(remote(a, a, g3s.at[i, 2 + q, 0], g3r.at[i, 2 + q, 0], dev))
-                copies.append(remote(b, b, g3s.at[i, 2 + q, 1], g3r.at[i, 2 + q, 1], dev))
+            n = 2 * which + q
+            copies.append(remote(a, a, g3s.at[i, n, 0], g3r.at[i, n, 0], at(axis_a, step)))
+            copies.append(remote(b, b, g3s.at[i, n, 1], g3r.at[i, n, 1], at(axis_b, step)))
         return copies
 
     g1 = [gather_copies(0, i) for i in range(3)]
@@ -195,9 +197,6 @@
     def a4_own(b):
         src, dst = a4_refs(b, ten)
         return pltpu.make_async_copy(src, dst, a4s.at[b, 0])
-
-    for c in ins:
-        c.wait()
 
     def first(k):
         def block(a):
@@ -219,12 +218,14 @@
         a1_own(k).start()
         loop(1, 16, lambda r: a1_copy(k, r).start())
 
-    first(0)
     pl.semaphore_wait(barrier, 23)
     for c in wins:
         c.wait()
     for i in range(3):
         start(g1[i])
+    for c in ins:
+        c.wait()
+    first(0)
     sc_t[...] = jnp.broadcast_to(sc_v[pl.ds(ten, 1), :], (LANES, LANES)).T
     sh_t[...] = jnp.broadcast_to(sh_v[pl.ds(ten, 1), :], (LANES, LANES)).T
     f2_b[...] = f2_v[...].astype(bf16)
@@ -298,7 +299,7 @@
 
     def mlp(i, blocks):
         for q, (which, b) in enumerate(blocks):
-            product = jnp.dot(we_all[i], n_all[which, b], preferred_element_type=f32)
+            product = jnp.dot(we_all[i].reshape(1024, 1024), n_all[which, b], preferred_element_type=f32)
             h_buf[q] = jax.nn.gelu(product).astype(bf16)
         return [jnp.dot(wr_t[i], h_buf[q], preferred_element_type=f32) for q in range(2)]
 
@@ -351,8 +352,8 @@
     finish(0)
     def tail(b):
         middle(b)
+        finish(b - 1)
         last(b)
-        finish(b - 1)
     loop(2, NT, tail)
     finish(NT - 1)
 
@@ -378,7 +379,7 @@
         vmem((128, 8192), bf16), vmem((512, 512), bf16), vmem((128, 8192), f32), vmem((256, 256), f32),
         vmem((256, 256), bf16), vmem((8, 128), f32), vmem((8, 128), f32),
         vmem((128, 128), f32), vmem((128, 128), f32),
-        vmem((3, 1024, 1024), bf16), vmem((3, 4, 4, 16, 1024), bf16), vmem((3, 1024, 1024), bf16),
+        vmem((3, 4, 4, 4, 16, 1024), bf16), vmem((3, 4, 4, 16, 1024), bf16), vmem((3, 1024, 1024), bf16),
         vmem((W // 128, 2048, 128), f32),
         vmem((NK, 128, 16, W), bf16), vmem((NK, 8, 256, W), bf16),
         vmem((NK, 8, 256, W), bf16), vmem((NK, 128, 16, W), bf16),

time: 169 us -> 160 us (0.947)
  the two profiles are of different devices: /device:TPU:108 before, /device:TPU:24 now
where the time goes in v3:
time: 160 us
  Pallas kernels  156 us (98%)
  local copies, waits for them, and re-layouts  3.1 us (2%)
    pallas_call x1, Pallas kernels, on_device(): pl.pallas_call(kernel, out_shape=jax.ShapeDtypeStruct((128, 8192), bf16),...  156 us

profile of v3, /device:TPU:24, one launch (start us, length us, event | category | flops | bytes accessed | tf_op | source)
XLA Modules:
  0.0 159.6 jit_solution(10884590998435655632)
XLA Ops:
  0.0 156.5 %mixer.1 = bf16[128,8192]{1,0:T(8,128)(2,1)} custom-call(bf16[128,8192]{1,0:T(8,128)(2,1)} %act.1, bf16[512,512]{1,0:T(8,128)(2,1)} %f1.1, f32[128,8192]{1,0:T(8,128)} %spec.1, f32[256,256]{1,0:T(8,128)} %f2.1, f32[8,128]{1,0:T(8,128)} %bitcast.4, f32[8,128]{1,0:T(8,128)} %bitcast.5, bf16[48,1024]{1,0:T(8,128)(2,1)} %bitcast.3, bf16[48,1024]{1,0:T(8,128)(2,1)} %wr.1), custom_call_target="tpu_custom_call" | custom-call | tf_op jit(solution)/shard_map/mixer/pallas_call | solution.py:395
  156.5 3.1 %copy.10 = bf16[128,8192]{1,0:T(8,128)(2,1)} copy(bf16[128,8192]{1,0:T(8,128)(2,1)} %mixer.1) | data formatting | bytes 4194304

commit v4 on v3

--- a/solution.py
+++ b/solution.py
@@ -15,7 +15,7 @@
 LANES = 128
 ORDERS = (("y", "z", "x"), ("y", "x", "z"), ("y", "z", "x"))
 WE_PATHS = (("y", "z", "x"), ("y", "x", "z"), ("z", "x", "y"))
-WR_PATHS = (("z", "y", "x"), ("y", "x", "z"), ("y", "z", "x"))
+WR_PATHS = (("z", "y", "x"), ("y", "x", "z"), ("z", "y", "x"))
 epsilon = 1e-06
 f32, bf16 = jnp.float32, jnp.bfloat16
 
@@ -215,6 +215,8 @@
                 rows = x32[g, pl.ds(pl.multiple_of(c * 16, 128), 128), :]
                 s_send[k, pl.ds(c, 8), :, g * LANES:(g + 1) * LANES] = rows.astype(bf16).reshape(8, 16, LANES)
         loop(0, 16, cast)
+
+    def send(k):
         a1_own(k).start()
         loop(1, 16, lambda r: a1_copy(k, r).start())
 
@@ -231,7 +233,9 @@
     f2_b[...] = f2_v[...].astype(bf16)
 
     send_first(0)
+    send(0)
     first(1)
+    send_first(1)
     for i in range(3):
         arrive(g1[i])
         start(g2[i])
@@ -239,23 +243,11 @@
     def mixing(k):
         a1_own(k).wait()
         loop(1, 16, lambda r: a1_copy(k, r).wait_recv())
-        if k == 0:
-            send_first(1)
         def mix(c):
             m_send[k, c] = jnp.dot(f2_b[...], s_recv[k, c], preferred_element_type=f32).astype(bf16)
         loop(0, 8, mix)
         a2_own(k).start()
         loop(1, 16, lambda r: a2_copy(k, r).start())
-
-    mixing(0)
-    arrive(g2[0])
-    turn(0)
-    start(g3[0])
-    mixing(1)
-    for i in (1, 2):
-        arrive(g2[i])
-        turn(i)
-        start(g3[i])
 
     def gating(k):
         a2_own(k).wait()
@@ -277,10 +269,19 @@
         a3_own(k).start()
         loop(1, 8, lambda r: a3_copy(k, r).start())
 
+    mixing(0)
+    arrive(g2[0])
+    turn(0)
+    start(g3[0])
+    send(1)
+    for i in (1, 2):
+        arrive(g2[i])
+        turn(i)
+        start(g3[i])
     gating(0)
+    mixing(1)
     arrive(g3[0])
     start(g4[0])
-    gating(1)
 
     def norm_copy(b):
         return remote(n_all.at[0, b], n_all.at[1, b], ns.at[b], nr.at[b], partner)
@@ -332,27 +333,28 @@
         loop(2 * k, 2 * k + 2, normalize)
 
     settle(0)
-    arrive(g3[1])
-    start(g4[1])
+    for i in (1, 2):
+        arrive(g3[i])
+        start(g4[i])
+    gating(1)
     arrive(g4[0])
     loop(0, 1, lambda n: opening(0, n))
     loop(0, 2, lambda b: norm_copy(b).wait_recv())
     loop(0, 1, lambda n: opening(1, n))
-    arrive(g3[2])
-    start(g4[2])
+    arrive(g4[1])
+    loop(0, 2, middle)
+    arrive(g4[2])
+    loop(0, 2, last)
     settle(1)
+    loop(0, 2, finish)
     loop(1, 2, lambda n: opening(0, n))
     loop(2, 4, lambda b: norm_copy(b).wait_recv())
     loop(1, 2, lambda n: opening(1, n))
-    arrive(g4[1])
-    loop(0, 2, middle)
-    arrive(g4[2])
-    last(0)
-    last(1)
-    finish(0)
     def tail(b):
         middle(b)
-        finish(b - 1)
+        @pl.when(b > 2)
+        def _():
+            finish(b - 1)
         last(b)
     loop(2, NT, tail)
     finish(NT - 1)

time: 160 us -> 158 us (0.988)
  the two profiles are of different devices: /device:TPU:24 before, /device:TPU:108 now
where the time goes in v4:
time: 158 us
  Pallas kernels  155 us (98%)
  local copies, waits for them, and re-layouts  3.1 us (2%)
    pallas_call x1, Pallas kernels, on_device(): pl.pallas_call(kernel, out_shape=jax.ShapeDtypeStruct((128, 8192), bf16),...  155 us

profile of v4, /device:TPU:108, one launch (start us, length us, event | category | flops | bytes accessed | tf_op | source)
XLA Modules:
  0.0 157.6 jit_solution(1310973830233475176)
XLA Ops:
  0.0 154.5 %mixer.1 = bf16[128,8192]{1,0:T(8,128)(2,1)} custom-call(bf16[128,8192]{1,0:T(8,128)(2,1)} %act.1, bf16[512,512]{1,0:T(8,128)(2,1)} %f1.1, f32[128,8192]{1,0:T(8,128)} %spec.1, f32[256,256]{1,0:T(8,128)} %f2.1, f32[8,128]{1,0:T(8,128)} %bitcast.4, f32[8,128]{1,0:T(8,128)} %bitcast.5, bf16[48,1024]{1,0:T(8,128)(2,1)} %bitcast.3, bf16[48,1024]{1,0:T(8,128)(2,1)} %wr.1), custom_call_target="tpu_custom_call" | custom-call | tf_op jit(solution)/shard_map/mixer/pallas_call | solution.py:397
  154.5 3.1 %copy.10 = bf16[128,8192]{1,0:T(8,128)(2,1)} copy(bf16[128,8192]{1,0:T(8,128)(2,1)} %mixer.1) | data formatting | bytes 4194304

commit v5 on v4

--- a/solution.py
+++ b/solution.py
@@ -332,10 +332,11 @@
         loop(1, 8, lambda r: a3_copy(k, r).wait_recv())
         loop(2 * k, 2 * k + 2, normalize)
 
+    arrive(g3[1])
+    start(g4[1])
     settle(0)
-    for i in (1, 2):
-        arrive(g3[i])
-        start(g4[i])
+    arrive(g3[2])
+    start(g4[2])
     gating(1)
     arrive(g4[0])
     loop(0, 1, lambda n: opening(0, n))

time: 158 us -> 158 us (level)
  no operation moved by 1% of the time
where the time goes in v5:
time: 158 us
  Pallas kernels  155 us (98%)
  local copies, waits for them, and re-layouts  3.1 us (2%)
    pallas_call x1, Pallas kernels, on_device(): pl.pallas_call(kernel, out_shape=jax.ShapeDtypeStruct((128, 8192), bf16),...  155 us

profile of v5, /device:TPU:108, one launch (start us, length us, event | category | flops | bytes accessed | tf_op | source)
XLA Modules:
  0.0 157.6 jit_solution(585731820793074147)
XLA Ops:
  0.0 154.5 %mixer.1 = bf16[128,8192]{1,0:T(8,128)(2,1)} custom-call(bf16[128,8192]{1,0:T(8,128)(2,1)} %act.1, bf16[512,512]{1,0:T(8,128)(2,1)} %f1.1, f32[128,8192]{1,0:T(8,128)} %spec.1, f32[256,256]{1,0:T(8,128)} %f2.1, f32[8,128]{1,0:T(8,128)} %bitcast.4, f32[8,128]{1,0:T(8,128)} %bitcast.5, bf16[48,1024]{1,0:T(8,128)(2,1)} %bitcast.3, bf16[48,1024]{1,0:T(8,128)(2,1)} %wr.1), custom_call_target="tpu_custom_call" | custom-call | tf_op jit(solution)/shard_map/mixer/pallas_call | solution.py:398
  154.5 3.1 %copy.10 = bf16[128,8192]{1,0:T(8,128)(2,1)} copy(bf16[128,8192]{1,0:T(8,128)(2,1)} %mixer.1) | data formatting | bytes 4194304
